TPU v7x, 128 devices: a whole 4x4x4 slice. The times are simulated.
128 devices in a mesh: member: 2 (over y_hi), gridy: 8 (over x, core), gridx: 8 (over z, y_lo).
Axes of the slice: x: 4, y: 4 (y_hi: 2, y_lo: 2; y = y_hi * 2 + y_lo), z: 4, core: 2. Of those that a mesh axis runs over, the one named last changes fastest.
Arguments:
- temp: float32 [4, 4, 512, 2048], P('member', None, 'gridy', 'gridx'), may hold values from -6 to 6
- salt: float32 [4, 4, 512, 2048], P('member', None, 'gridy', 'gridx'), may hold values from -6 to 6
- uvel: float32 [4, 4, 512, 2048], P('member', None, 'gridy', 'gridx'), may hold values from -3 to 3
- vvel: float32 [4, 4, 512, 2048], P('member', None, 'gridy', 'gridx'), may hold values from -3 to 3
- eta: float32 [4, 512, 2048], P('member', 'gridy', 'gridx'), may hold values from -6 to 6
- land_mask: int32 [512, 2048], P('gridy', 'gridx'), may hold values 0 or 1
- clone_source: int32 [4], P('member'), may hold values from 0 to 3
Outputs:
- new_temp: float32 [4, 4, 512, 2048], P('member', None, 'gridy', 'gridx')
- new_salt: float32 [4, 4, 512, 2048], P('member', None, 'gridy', 'gridx')
- new_uvel: float32 [4, 4, 512, 2048], P('member', None, 'gridy', 'gridx')
- new_vvel: float32 [4, 4, 512, 2048], P('member', None, 'gridy', 'gridx')
- new_eta: float32 [4, 512, 2048], P('member', 'gridy', 'gridx')
- overturning: float32 [4, 4, 512], P('member', None, 'gridy')
- clone_weight: float32 [4], P('member')
All inputs are finite; a program needn't handle non-finite values. No bound on the sum of `land_mask` on one device may be relied on, other than what follows from the above.
Results may differ from a plain program's by a relative error of at most 0.0001.
Values sent between devices are 32-bit elements; how exact they have to be, the bound alone decides.
A program may use at most 128 MiB of HBM per device.

v0:
```python
import jax
import jax.numpy as jnp
from jax import lax
from jax.sharding import PartitionSpec as P

STEPS = 2
ITERS = 3
ALPHA_T = 0.8
BETA_S = 0.6
PRESS_K = 0.25
STEP_DT = 0.1
KAPPA = 0.1
VISCOSITY = 0.1
DRAG_K = 0.05
CORI_K = 1.0
SURF_C = 4.0
DIV_K = 0.5
GRAV_K = 0.5


def padded_2(block, sides, width):
    for axis, dim in sides:
        count = lax.axis_size(axis)
        forward = [(i, i + 1) for i in range(count - 1)]
        forward.append((count - 1, 0))
        backward = [(target, source) for source, target in forward]
        low = lax.ppermute(
            lax.slice_in_dim(block, block.shape[dim] - width, None, axis=dim), axis, forward
        )
        high = lax.ppermute(lax.slice_in_dim(block, 0, width, axis=dim), axis, backward)
        block = jnp.concatenate([low, block, high], axis=dim)
    return block


def pressure(temp, salt):
    return PRESS_K * jnp.cumsum(BETA_S * salt - ALPHA_T * temp, axis=-3)


def split_rims(padded, south_keep, north_keep):
    east_side = padded[..., 1:-1, 2:]
    west_side = padded[..., 1:-1, :-2]
    north_side = padded[..., 2:, 1:-1]
    south_side = padded[..., :-2, 1:-1]
    north_side = north_side.at[..., -1, :].multiply(north_keep)
    south_side = south_side.at[..., 0, :].multiply(south_keep)
    return (east_side, west_side, north_side, south_side)


def volume_sides(fields, south_keep, north_keep):
    padded = padded_2(jnp.stack(fields), (("gridy", 3), ("gridx", 4)), 1)
    return split_rims(padded, south_keep, north_keep)


def surface_sides(fields, south_keep, north_keep):
    padded = padded_2(jnp.stack(fields), (("gridy", 2), ("gridx", 3)), 1)
    return split_rims(padded, south_keep, north_keep)


def surface_apply(field, south_keep, north_keep):
    east_side, west_side, north_side, south_side = surface_sides((field,), south_keep, north_keep)
    return (1.0 + 4.0 * SURF_C) * field - SURF_C * (
        east_side[0] + west_side[0] + north_side[0] + south_side[0]
    )


def member_total(values):
    return jnp.sum(values, axis=(1, 2))


def squared_norm(residual):
    return lax.psum(member_total(residual * residual), ("gridy", "gridx"))


def widen(values):
    return values[:, None, None]


def surface_solve(rhs, south_keep, north_keep):
    solution = jnp.zeros_like(rhs)
    residual = rhs
    direction = rhs
    norm_now = squared_norm(residual)
    for count in range(ITERS):
        image = surface_apply(direction, south_keep, north_keep)
        alpha = norm_now / lax.psum(member_total(direction * image), ("gridy", "gridx"))
        solution = solution + widen(alpha) * direction
        residual = residual - widen(alpha) * image
        norm_next = squared_norm(residual)
        direction = residual + widen(norm_next / norm_now) * direction
        norm_now = norm_next
    return solution


def shards(temp, salt, uvel, vvel, eta, land_mask, clone_source):
    levels = temp.shape[1]
    rows = temp.shape[2]
    cols = temp.shape[3]
    ocean = land_mask.astype(jnp.float32)
    tile_row = lax.axis_index("gridy")
    tile_count = lax.axis_size("gridy")
    total_rows = rows * tile_count
    total_cols = cols * lax.axis_size("gridx")
    south_keep = (tile_row > 0).astype(jnp.float32)
    north_keep = (tile_row < tile_count - 1).astype(jnp.float32)
    latitude = (tile_row * rows + jnp.arange(rows, dtype=jnp.int32)).astype(jnp.float32) + 0.5
    coriolis = (CORI_K * (2.0 * latitude / total_rows - 1.0))[:, None]
    for count in range(STEPS):
        press = pressure(temp, salt)
        east_side, west_side, north_side, south_side = volume_sides(
            (temp, salt, uvel, vvel, press), south_keep, north_keep
        )
        lap_temp = east_side[0] + west_side[0] + north_side[0] + south_side[0] - 4.0 * temp
        lap_salt = east_side[1] + west_side[1] + north_side[1] + south_side[1] - 4.0 * salt
        lap_uvel = east_side[2] + west_side[2] + north_side[2] + south_side[2] - 4.0 * uvel
        lap_vvel = east_side[3] + west_side[3] + north_side[3] + south_side[3] - 4.0 * vvel
        temp_next = ocean * (
            temp
            - STEP_DT
            * 0.5
            * (uvel * (east_side[0] - west_side[0]) + vvel * (north_side[0] - south_side[0]))
            + KAPPA * lap_temp
        )
        salt_next = ocean * (
            salt
            - STEP_DT
            * 0.5
            * (uvel * (east_side[1] - west_side[1]) + vvel * (north_side[1] - south_side[1]))
            + KAPPA * lap_salt
        )
        ustar = ocean * (
            uvel
            + STEP_DT * (coriolis * vvel - 0.5 * (east_side[4] - west_side[4]) - DRAG_K * uvel)
            + VISCOSITY * lap_uvel
        )
        vstar = ocean * (
            vvel
            + STEP_DT * (-coriolis * uvel - 0.5 * (north_side[4] - south_side[4]) - DRAG_K * vvel)
            + VISCOSITY * lap_vvel
        )
        trans_u = jnp.sum(ustar, axis=1)
        trans_v = jnp.sum(vstar, axis=1)
        east_t, west_t, north_t, south_t = surface_sides((trans_u, trans_v), south_keep, north_keep)
        rhs = eta - DIV_K * 0.5 * (east_t[0] - west_t[0] + (north_t[1] - south_t[1]))
        eta = surface_solve(rhs, south_keep, north_keep)
        east_e, west_e, north_e, south_e = surface_sides((eta,), south_keep, north_keep)
        uvel = ocean * (ustar - GRAV_K * 0.5 * (east_e[0] - west_e[0])[:, None])
        vvel = ocean * (vstar - GRAV_K * 0.5 * (north_e[0] - south_e[0])[:, None])
        temp = temp_next
        salt = salt_next
    zonal_scale = 1.0 / jnp.sqrt(jnp.float32(total_cols))
    score_scale = 1.0 / jnp.sqrt(jnp.float32(levels * total_rows))
    lat_weight = latitude / total_rows
    zonal_local = jnp.sum(vvel, axis=3)
    zonal_whole = lax.psum(zonal_local, "gridx")
    overturn = jnp.cumsum(zonal_whole, axis=1) * zonal_scale
    score = lax.psum(jnp.sum(overturn * lat_weight, axis=(1, 2)) * score_scale, "gridy")
    state_stack = jnp.stack((temp, salt, uvel, vvel))
    every_state, every_eta, every_score = (
        lax.all_gather(state_stack, "member", axis=1, tiled=True),
        lax.all_gather(eta, "member", axis=0, tiled=True),
        lax.all_gather(score, "member", axis=0, tiled=True),
    )
    picked = jnp.take(every_state, clone_source, axis=1)
    new_eta = jnp.take(every_eta, clone_source, axis=0)
    clone_weight = jnp.take(every_score, clone_source, axis=0) - jnp.mean(every_score)
    return (picked[0], picked[1], picked[2], picked[3], new_eta, overturn, clone_weight)


def solution(mesh):
    in_specs = (
        P("member", None, "gridy", "gridx"),
        P("member", None, "gridy", "gridx"),
        P("member", None, "gridy", "gridx"),
        P("member", None, "gridy", "gridx"),
        P("member", "gridy", "gridx"),
        P("gridy", "gridx"),
        P("member"),
    )
    out_specs = (
        P("member", None, "gridy", "gridx"),
        P("member", None, "gridy", "gridx"),
        P("member", None, "gridy", "gridx"),
        P("member", None, "gridy", "gridx"),
        P("member", "gridy", "gridx"),
        P("member", None, "gridy"),
        P("member"),
    )
    return jax.shard_map(shards, mesh=mesh, in_specs=in_specs, out_specs=out_specs, check_vma=False)
```

profile of v0, /device:TPU:1, one launch (start us, length us, event | category | flops | bytes accessed | tf_op | source)
XLA Modules:
  0.0 1724.0 jit_solution(7264022242541431259)
XLA Ops:
  15.9 2.1 fusion.186
  18.0 1.9 copy.16
  21.2 1.9 copy.14
  23.1 3.5 collective-permute-start.2
  26.7 3.0 pad_maximum_fusion.5
  29.8 2.2 scatter-mul.81
  32.0 2.2 scatter-mul.80
  37.6 2.9 fusion.179
  40.7 2.9 fusion.181
  43.6 4.2 collective-permute-start.5
  49.2 3.6 collective-permute-start.6
  52.9 2.3 collective-permute-done.7
  57.2 3.4 collective-permute-start.9
  62.0 3.9 collective-permute-start.10
  68.0 133.2 %all-reduce.2 = (f32[2]{0:T(128)S(1)}, f32[2]{0:T(128)S(1)}) all-reduce(f32[2]{0:T(128)S(1)} %get-tuple-element.298, f32[2]{0:T(128)S(1)} %get-tuple-element.297), channel_id=1, replica_groups=mesh['member'=2,'gridy'=8,'gridx'=8] {'gridy','gridx'}, use_global_device_ids=true, to_apply=%region_4.5 | all-reduce | flops 4 | bytes 32 | tf_op jit(solution)/shard_map/psum | solution.py:71
  201.4 139.0 %psum.100 = f32[2]{0:T(128)S(1)} all-reduce(f32[2]{0:T(128)S(1)} %get-tuple-element.316), channel_id=1, replica_groups=mesh['member'=2,'gridy'=8,'gridx'=8] {'gridy','gridx'}, use_global_device_ids=true, to_apply=%region_8.9 | all-reduce | flops 2 | bytes 16 | tf_op jit(solution)/shard_map/psum | solution.py:71
  340.5 11.4 collective-permute-start.13
  354.9 1.8 collective-permute-start.14
  358.8 133.5 %psum.101 = f32[2]{0:T(128)S(1)} all-reduce(f32[2]{0:T(128)S(1)} %get-tuple-element.314), channel_id=1, replica_groups=mesh['member'=2,'gridy'=8,'gridx'=8] {'gridy','gridx'}, use_global_device_ids=true, to_apply=%region_10.11 | all-reduce | flops 2 | bytes 16 | tf_op jit(solution)/shard_map/psum | solution.py:85
  492.5 139.0 %psum.102 = f32[2]{0:T(128)S(1)} all-reduce(f32[2]{0:T(128)S(1)} %multiply_reduce_fusion.5), channel_id=1, replica_groups=mesh['member'=2,'gridy'=8,'gridx'=8] {'gridy','gridx'}, use_global_device_ids=true, to_apply=%region_12.13 | all-reduce | flops 2 | bytes 16 | tf_op jit(solution)/shard_map/psum | solution.py:71
  632.1 11.4 collective-permute-start.17
  644.8 1.9 collective-permute-start.19
  651.0 3.5 bitcast_dynamic-update-slice_fusion.3
  654.5 134.3 %psum.103 = f32[2]{0:T(128)} all-reduce(f32[2]{0:T(128)} %fusion.143), channel_id=1, replica_groups=mesh['member'=2,'gridy'=8,'gridx'=8] {'gridy','gridx'}, use_global_device_ids=true, to_apply=%region_14.15 | all-reduce | flops 2 | bytes 16 | tf_op jit(solution)/shard_map/psum | solution.py:85
  790.5 11.7 collective-permute-start.21
  802.2 3.5 bitcast_dynamic-update-slice_fusion.2
  805.9 3.6 collective-permute-start.22
  816.5 4.1 collective-permute-start.25
  822.3 2.1 fusion.185
  824.4 2.5 copy.20
  826.9 2.5 copy.18
  829.4 3.9 collective-permute-start.26
  833.2 3.0 pad_maximum_fusion.3
  837.5 2.2 scatter-mul.101
  839.7 2.2 scatter-mul.100
  841.9 2.4 copy.21
  844.3 2.5 copy.19
  846.8 3.4 fusion.175
  850.3 3.0 fusion.173
  853.3 3.7 collective-permute-start.29
  859.0 3.6 collective-permute-start.30
  867.7 3.6 collective-permute-start.33
  873.2 3.6 collective-permute-start.34
  881.4 1.8 multiply_reduce_fusion.3
  883.2 131.9 %all-reduce.1 = (f32[2]{0:T(128)}, f32[2]{0:T(128)}) all-reduce(f32[2]{0:T(128)} %get-tuple-element.296, f32[2]{0:T(128)} %get-tuple-element.295), channel_id=1, replica_groups=mesh['member'=2,'gridy'=8,'gridx'=8] {'gridy','gridx'}, use_global_device_ids=true, to_apply=%region_19.20 | all-reduce | flops 4 | bytes 32 | tf_op jit(solution)/shard_map/psum | solution.py:71
  1017.1 140.1 %psum.106 = f32[2]{0:T(128)S(1)} all-reduce(f32[2]{0:T(128)} %get-tuple-element.307), channel_id=1, replica_groups=mesh['member'=2,'gridy'=8,'gridx'=8] {'gridy','gridx'}, use_global_device_ids=true, to_apply=%region_23.24 | all-reduce | flops 2 | bytes 16 | tf_op jit(solution)/shard_map/psum | solution.py:71
  1158.9 11.7 collective-permute-start.37
  1172.7 3.4 collective-permute-start.38
  1180.7 2.4 multiply_reduce_fusion.1
  1183.0 131.7 %psum.107 = f32[2]{0:T(128)} all-reduce(f32[2]{0:T(128)} %get-tuple-element.305), channel_id=1, replica_groups=mesh['member'=2,'gridy'=8,'gridx'=8] {'gridy','gridx'}, use_global_device_ids=true, to_apply=%region_25.26 | all-reduce | flops 2 | bytes 16 | tf_op jit(solution)/shard_map/psum | solution.py:85
  1317.6 141.2 %psum.108 = f32[2]{0:T(128)} all-reduce(f32[2]{0:T(128)} %multiply_reduce_fusion), channel_id=1, replica_groups=mesh['member'=2,'gridy'=8,'gridx'=8] {'gridy','gridx'}, use_global_device_ids=true, to_apply=%region_27.28 | all-reduce | flops 2 | bytes 16 | tf_op jit(solution)/shard_map/psum | solution.py:71
  1460.6 11.8 collective-permute-start.41
  1474.3 3.6 collective-permute-start.42
  1482.5 2.0 fusion.107
  1484.5 131.7 %psum.109 = f32[2]{0:T(128)} all-reduce(f32[2]{0:T(128)} %fusion.107), channel_id=1, replica_groups=mesh['member'=2,'gridy'=8,'gridx'=8] {'gridy','gridx'}, use_global_device_ids=true, to_apply=%region_29.30 | all-reduce | flops 2 | bytes 16 | tf_op jit(solution)/shard_map/psum | solution.py:85
  1617.8 11.5 collective-permute-start.45
  1639.8 3.4 fusion.87
  1643.2 1.9 fusion.50
  1648.0 16.1 psum.110
  1664.8 9.2 all_gather.10
  1674.0 21.4 %psum.111 = f32[2]{0:T(128)S(1)} all-reduce(f32[2]{0:T(128)S(1)} %broadcast_multiply_fusion.9), channel_id=1, replica_groups=mesh['member'=2,'gridy'=8,'gridx'=8] {'gridy'}, use_global_device_ids=true, to_apply=%region_34.35 | all-reduce | flops 2 | bytes 16 | tf_op jit(solution)/shard_map/psum | solution.py:156
  1696.2 5.8 all-reduce
  1705.1 7.6 all-gather.2.cloned.1.call-done
  1712.7 2.9 gather_fusion
  (325 shorter events, 98.7 us)
Async XLA Ops:
  7.2 1705.5 %all-gather.2.cloned.1.call-start = ((), (), s32[]{:S(2)}) async-start(), calls=%async_computation | async-start | bytes 6291456 | tf_op jit(solution)/shard_map/all_gather | solution.py:159
  11.0 29.6 %copy-start = (f32[5,2,4,64,256]{4,3,2,1,0:T(8,128)}, f32[5,2,4,64,256]{4,3,2,1,0:T(8,128)S(1)}, u32[]{:S(2)}) copy-start(f32[5,2,4,64,256]{4,3,2,1,0:T(8,128)S(1)} %constant_dynamic-update-slice_fusion) | copy-start | bytes 7864324
  11.0 4.3 collective-permute-start.1
  12.5 3.0 collective-permute-start
  14.2 23.4 %copy-start.44 = (f32[64]{0:T(128)}, f32[64]{0:T(128)S(1)}, u32[]{:S(2)}) copy-start(f32[64]{0:T(128)S(1)} %get-tuple-element.412) | copy-start | bytes 772
  19.9 14.3 collective-permute-start.3
  23.1 12.8 collective-permute-start.2
  43.6 11.7 copy-start.25
  43.6 5.0 collective-permute-start.5
  47.8 1.2 collective-permute-start.4
  49.1 6.2 collective-permute-start.7
  49.2 6.9 collective-permute-start.6
  57.2 4.2 collective-permute-start.9
  60.6 1.2 collective-permute-start.8
  61.9 5.7 collective-permute-start.11
  62.0 5.7 collective-permute-start.10
  201.2 139.2 %copy-start.47 = (f32[2]{0:T(128)}, f32[2]{0:T(128)S(1)}, u32[]{:S(2)}) copy-start(f32[2]{0:T(128)S(1)} %div.41) | copy-start | bytes 28
  340.5 12.2 collective-permute-start.13
  351.9 1.2 collective-permute-start.12
  353.1 5.4 collective-permute-start.15
  354.9 3.6 collective-permute-start.14
  492.3 152.5 %copy-start.42 = (f32[2]{0:T(128)}, f32[2]{0:T(128)S(1)}, u32[]{:S(2)}) copy-start(f32[2]{0:T(128)S(1)} %div.43) | copy-start | bytes 28
  632.1 18.1 %copy-start.12 = (f32[2,64,256]{2,1,0:T(8,128)}, f32[2,64,256]{2,1,0:T(8,128)S(1)}, u32[]{:S(2)}) copy-start(f32[2,64,256]{2,1,0:T(8,128)S(1)} %multiply_add_fusion.4) | copy-start | bytes 393220
  632.1 12.2 collective-permute-start.17
  643.5 1.2 collective-permute-start.16
  644.8 5.4 collective-permute-start.19
  646.7 3.5 collective-permute-start.18
  790.4 20.8 %copy-start.26 = (f32[2,64,256]{2,1,0:T(8,128)}, f32[2,64,256]{2,1,0:T(8,128)S(1)}, u32[]{:S(2)}) copy-start(f32[2,64,256]{2,1,0:T(8,128)S(1)} %multiply_add_fusion.3) | copy-start | bytes 393220
  790.4 15.3 collective-permute-start.20
  790.5 15.2 collective-permute-start.21
  805.8 5.4 collective-permute-start.23
  805.9 5.3 collective-permute-start.22
  811.9 38.3 %copy-start.16 = (f32[2,64,256]{2,1,0:T(8,128)}, f32[2,64,256]{2,1,0:T(8,128)S(1)}, u32[]{:S(2)}) copy-start(f32[2,64,256]{2,1,0:T(8,128)S(1)} %get-tuple-element.377) | copy-start | bytes 393220
  815.1 35.2 %copy-start.14 = (f32[2,64,256]{2,1,0:T(8,128)}, f32[2,64,256]{2,1,0:T(8,128)S(1)}, u32[]{:S(2)}) copy-start(f32[2,64,256]{2,1,0:T(8,128)S(1)} %subtract_multiply_fusion.4) | copy-start | bytes 393220
  816.5 5.0 collective-permute-start.25
  820.6 1.2 collective-permute-start.24
  826.9 15.0 collective-permute-start.27
  829.4 14.9 collective-permute-start.26
  850.2 12.3 copy-start.23
  853.3 10.2 copy-start.24
  853.3 4.6 collective-permute-start.29
  857.0 1.2 collective-permute-start.28
  859.0 7.2 collective-permute-start.31
  859.0 7.3 collective-permute-start.30
  867.7 4.5 collective-permute-start.33
  871.3 1.2 collective-permute-start.32
  873.2 7.6 collective-permute-start.35
  873.2 8.2 collective-permute-start.34
  1158.9 12.5 collective-permute-start.37
  1170.6 1.2 collective-permute-start.36
  1172.5 8.1 collective-permute-start.39
  1172.7 8.0 collective-permute-start.38
  1460.6 18.4 %copy-start.13 = (f32[2,64,256]{2,1,0:T(8,128)}, f32[2,64,256]{2,1,0:T(8,128)S(1)}, u32[]{:S(2)}) copy-start(f32[2,64,256]{2,1,0:T(8,128)S(1)} %multiply_add_fusion.1) | copy-start | bytes 393220
  1460.6 12.6 collective-permute-start.41
  1472.4 1.2 collective-permute-start.40
  1473.2 6.5 copy-start.37
  1474.3 8.2 collective-permute-start.43
  1474.3 8.2 collective-permute-start.42
  1617.8 18.1 %copy-start.27 = (f32[2,64,256]{2,1,0:T(8,128)}, f32[2,64,256]{2,1,0:T(8,128)S(1)}, u32[]{:S(2)}) copy-start(f32[2,64,256]{2,1,0:T(8,128)S(1)} %multiply_add_fusion) | copy-start | bytes 393220
  1617.8 12.3 collective-permute-start.45
  1629.3 1.2 collective-permute-start.44
  1630.6 5.4 collective-permute-start.47
  1632.4 3.6 collective-permute-start.46
  1645.2 19.6 %copy-start.28 = (f32[2,64,256]{2,1,0:T(8,128)S(1)}, f32[2,64,256]{2,1,0:T(8,128)}, u32[]{:S(2)}) copy-start(f32[2,64,256]{2,1,0:T(8,128)} %copy-done.27) | copy-start | bytes 393220
  (38 other events, 119.4 us)
Sparse Core Ops, SparseCore 0:
  1646.8 65.7 all-gather.1
where the time goes:
time: 1730 us; the launch traced here: 1720 us
  blocking collectives  1410 us (82%)
  starting transfers between devices  137 us (8%)
  other arithmetic  72.2 us (4%)
  local copies, waits for them, and re-layouts  59.9 us (3%)
  waiting for transfers between devices  31 us (2%)
    psum x6, blocking collectives, squared_norm(): return lax.psum(member_total(residual * residual), ('gridy', 'gridx'))  825 us
    psum x4, blocking collectives, surface_solve(): lax.psum(member_total(direction * image), ('gridy', 'gridx'))  531 us
    ppermute x24, starting transfers between devices, padded_2(): lax.ppermute(lax.slice_in_dim(block, 0, width, axis=dim), axis, backward)  128 us
  transfers between devices with their start and end apart: 49, of which 31 were waited for; matrix products, arithmetic and copies ran while one was open for 3% of the time, Pallas kernels for 0%

commit v1 on v0

--- a/solution.py
+++ b/solution.py
@@ -1,3 +1,4 @@
+import functools
 import jax
 import jax.numpy as jnp
 from jax import lax
@@ -16,6 +17,13 @@
 SURF_C = 4.0
 DIV_K = 0.5
 GRAV_K = 0.5
+
+
+def remake_the_heaps(unit, link_axis, chip_axis):
+    return jax.lax.psum(jax.lax.psum(unit, axis_name=link_axis), axis_name=chip_axis)
+
+
+_draft_rounds = functools.partial(remake_the_heaps, link_axis="gridy", chip_axis="gridx")
 
 
 def padded_2(block, sides, width):
@@ -82,7 +90,7 @@
     norm_now = squared_norm(residual)
     for count in range(ITERS):
         image = surface_apply(direction, south_keep, north_keep)
-        alpha = norm_now / lax.psum(member_total(direction * image), ("gridy", "gridx"))
+        alpha = norm_now / _draft_rounds(member_total(direction * image))
         solution = solution + widen(alpha) * direction
         residual = residual - widen(alpha) * image
         norm_next = squared_norm(residual)

time: 1730 us -> 1350 us (0.78)
  blocking collectives: 1410 us -> 1050 us
    psum x4 -> x12, blocking collectives: 531 us -> 186 us  [the longest x6 96.6 us: remake_the_heaps(): jax.lax.psum(unit, axis_name=link_axis)]
  transfers between devices with their start and end apart: 49 -> 49, of which waited for: 31 -> 32; matrix products, arithmetic and copies ran while one was open for 3% -> 4% of each run, Pallas kernels for 0% -> 0%
where the time goes in v1:
time: 1350 us
  blocking collectives  1050 us (78%)
  starting transfers between devices  122 us (9%)
  other arithmetic  71.7 us (5%)
  local copies, waits for them, and re-layouts  59.9 us (4%)
  waiting for transfers between devices  31.6 us (2%)
  between operations  16.3 us (1%)
    psum x6, blocking collectives, squared_norm(): return lax.psum(member_total(residual * residual), ('gridy', 'gridx'))  810 us
    ppermute x24, starting transfers between devices, padded_2(): lax.ppermute(lax.slice_in_dim(block, 0, width, axis=dim), axis, backward)  111 us
    psum x6, blocking collectives, remake_the_heaps(): jax.lax.psum(unit, axis_name=link_axis)  96.6 us
    psum x6, blocking collectives, remake_the_heaps(): jax.lax.psum(jax.lax.psum(unit, axis_name=link_axis), axis_name=chip_axis)  89.8 us
  transfers between devices with their start and end apart: 49, of which 32 were waited for; matrix products, arithmetic and copies ran while one was open for 4% of the time, Pallas kernels for 0%

profile of v1, /device:TPU:1, one launch (start us, length us, event | category | flops | bytes accessed | tf_op | source)
XLA Modules:
  0.0 1351.3 jit_solution(705025263639422169)
XLA Ops:
  23.1 3.5 collective-permute-start.2
  26.7 3.0 pad_maximum_fusion.5
  29.8 2.2 scatter-mul.81
  32.0 2.2 scatter-mul.80
  37.7 2.9 fusion.179
  40.8 2.9 fusion.181
  43.7 4.2 collective-permute-start.5
  49.3 3.6 collective-permute-start.6
  53.0 2.3 collective-permute-done.7
  57.3 3.4 collective-permute-start.9
  62.1 3.9 collective-permute-start.10
  68.1 16.0 %psum.141 = f32[2]{0:T(128)S(1)} all-reduce(f32[2]{0:T(128)S(1)} %get-tuple-element.297), channel_id=1, replica_groups=mesh['member'=2,'gridy'=8,'gridx'=8] {'gridy'}, use_global_device_ids=true, to_apply=%region_6.7 | all-reduce | flops 2 | bytes 16 | tf_op jit(solution)/shard_map/psum | solution.py:23
  84.0 130.4 %psum.140 = f32[2]{0:T(128)S(1)} all-reduce(f32[2]{0:T(128)S(1)} %get-tuple-element.298), channel_id=1, replica_groups=mesh['member'=2,'gridy'=8,'gridx'=8] {'gridy','gridx'}, use_global_device_ids=true, to_apply=%region_4.5 | all-reduce | flops 2 | bytes 16 | tf_op jit(solution)/shard_map/psum | solution.py:79
  214.4 12.5 psum.142
  227.2 144.0 %psum.143 = f32[2]{0:T(128)S(1)} all-reduce(f32[2]{0:T(128)S(1)} %get-tuple-element.312), channel_id=1, replica_groups=mesh['member'=2,'gridy'=8,'gridx'=8] {'gridy','gridx'}, use_global_device_ids=true, to_apply=%region_9.10 | all-reduce | flops 2 | bytes 16 | tf_op jit(solution)/shard_map/psum | solution.py:79
  371.3 11.8 collective-permute-start.13
  384.4 3.6 collective-permute-start.14
  390.2 15.7 %psum.144 = f32[2]{0:T(128)S(1)} all-reduce(f32[2]{0:T(128)S(1)} %get-tuple-element.310), channel_id=1, replica_groups=mesh['member'=2,'gridy'=8,'gridx'=8] {'gridy'}, use_global_device_ids=true, to_apply=%region_11.12 | all-reduce | flops 2 | bytes 16 | tf_op jit(solution)/shard_map/psum | solution.py:23
  405.9 16.4 %psum.145 = f32[2]{0:T(128)S(1)} all-reduce(f32[2]{0:T(128)S(1)} %psum.144), channel_id=1, replica_groups=mesh['member'=2,'gridy'=8,'gridx'=8] {'gridx'}, use_global_device_ids=true, to_apply=%region_12.13 | all-reduce | flops 2 | bytes 16 | tf_op jit(solution)/shard_map/psum | solution.py:23
  422.5 131.1 %psum.146 = f32[2]{0:T(128)S(1)} all-reduce(f32[2]{0:T(128)S(1)} %multiply_reduce_fusion.5), channel_id=1, replica_groups=mesh['member'=2,'gridy'=8,'gridx'=8] {'gridy','gridx'}, use_global_device_ids=true, to_apply=%region_14.15 | all-reduce | flops 2 | bytes 16 | tf_op jit(solution)/shard_map/psum | solution.py:79
  554.3 11.7 collective-permute-start.17
  572.9 16.8 %psum.147 = f32[2]{0:T(128)} all-reduce(f32[2]{0:T(128)S(1)} %fusion.143), channel_id=1, replica_groups=mesh['member'=2,'gridy'=8,'gridx'=8] {'gridy'}, use_global_device_ids=true, to_apply=%region_16.17 | all-reduce | flops 2 | bytes 16 | tf_op jit(solution)/shard_map/psum | solution.py:23
  589.8 3.5 bitcast_dynamic-update-slice_fusion.3
  593.3 16.9 %psum.148 = f32[2]{0:T(128)} all-reduce(f32[2]{0:T(128)} %psum.147), channel_id=1, replica_groups=mesh['member'=2,'gridy'=8,'gridx'=8] {'gridx'}, use_global_device_ids=true, to_apply=%region_17.18 | all-reduce | flops 2 | bytes 16 | tf_op jit(solution)/shard_map/psum | solution.py:23
  611.8 2.6 collective-permute-start.20
  616.3 3.5 bitcast_dynamic-update-slice_fusion.2
  620.0 3.6 collective-permute-start.22
  630.6 4.1 collective-permute-start.25
  638.5 2.5 copy.20
  641.0 2.5 copy.18
  643.5 3.9 collective-permute-start.26
  647.3 3.0 pad_maximum_fusion.3
  651.6 2.2 scatter-mul.101
  653.8 2.2 scatter-mul.100
  656.0 2.4 copy.21
  658.4 2.5 copy.19
  660.9 3.4 fusion.175
  664.3 3.0 fusion.173
  667.4 3.7 collective-permute-start.29
  673.1 3.6 collective-permute-start.30
  681.8 3.7 collective-permute-start.33
  687.3 3.6 collective-permute-start.34
  697.3 16.0 %psum.150 = f32[2]{0:T(128)} all-reduce(f32[2]{0:T(128)} %get-tuple-element.295), channel_id=1, replica_groups=mesh['member'=2,'gridy'=8,'gridx'=8] {'gridy'}, use_global_device_ids=true, to_apply=%region_24.25 | all-reduce | flops 2 | bytes 16 | tf_op jit(solution)/shard_map/psum | solution.py:23
  713.3 129.5 %psum.149 = f32[2]{0:T(128)} all-reduce(f32[2]{0:T(128)} %get-tuple-element.296), channel_id=1, replica_groups=mesh['member'=2,'gridy'=8,'gridx'=8] {'gridy','gridx'}, use_global_device_ids=true, to_apply=%region_22.23 | all-reduce | flops 2 | bytes 16 | tf_op jit(solution)/shard_map/psum | solution.py:79
  842.8 13.5 psum.151
  858.2 143.9 %psum.152 = f32[2]{0:T(128)S(1)} all-reduce(f32[2]{0:T(128)} %get-tuple-element.303), channel_id=1, replica_groups=mesh['member'=2,'gridy'=8,'gridx'=8] {'gridy','gridx'}, use_global_device_ids=true, to_apply=%region_27.28 | all-reduce | flops 2 | bytes 16 | tf_op jit(solution)/shard_map/psum | solution.py:79
  1003.8 11.4 collective-permute-start.37
  1018.3 2.3 collective-permute-start.38
  1025.2 2.4 multiply_reduce_fusion.1
  1027.6 16.0 %psum.153 = f32[2]{0:T(128)} all-reduce(f32[2]{0:T(128)} %get-tuple-element.301), channel_id=1, replica_groups=mesh['member'=2,'gridy'=8,'gridx'=8] {'gridy'}, use_global_device_ids=true, to_apply=%region_29.30 | all-reduce | flops 2 | bytes 16 | tf_op jit(solution)/shard_map/psum | solution.py:23
  1043.6 15.3 %psum.154 = f32[2]{0:T(128)} all-reduce(f32[2]{0:T(128)} %psum.153), channel_id=1, replica_groups=mesh['member'=2,'gridy'=8,'gridx'=8] {'gridx'}, use_global_device_ids=true, to_apply=%region_30.31 | all-reduce | flops 2 | bytes 16 | tf_op jit(solution)/shard_map/psum | solution.py:23
  1061.8 131.6 %psum.155 = f32[2]{0:T(128)} all-reduce(f32[2]{0:T(128)} %multiply_reduce_fusion), channel_id=1, replica_groups=mesh['member'=2,'gridy'=8,'gridx'=8] {'gridy','gridx'}, use_global_device_ids=true, to_apply=%region_32.33 | all-reduce | flops 2 | bytes 16 | tf_op jit(solution)/shard_map/psum | solution.py:79
  1195.1 11.7 collective-permute-start.41
  1218.9 16.0 %psum.156 = f32[2]{0:T(128)} all-reduce(f32[2]{0:T(128)} %fusion.107), channel_id=1, replica_groups=mesh['member'=2,'gridy'=8,'gridx'=8] {'gridy'}, use_global_device_ids=true, to_apply=%region_34.35 | all-reduce | flops 2 | bytes 16 | tf_op jit(solution)/shard_map/psum | solution.py:23
  1235.0 15.3 %psum.157 = f32[2]{0:T(128)} all-reduce(f32[2]{0:T(128)} %psum.156), channel_id=1, replica_groups=mesh['member'=2,'gridy'=8,'gridx'=8] {'gridx'}, use_global_device_ids=true, to_apply=%region_35.36 | all-reduce | flops 2 | bytes 16 | tf_op jit(solution)/shard_map/psum | solution.py:23
  1251.9 4.2 collective-permute-start.45
  1257.5 3.6 collective-permute-start.46
  1266.7 3.4 fusion.87
  1274.9 16.6 %psum.158 = f32[2,4,64]{2,1,0:T(4,128)S(1)} all-reduce(f32[2,4,64]{2,1,0:T(4,128)S(1)} %copy-done.41), channel_id=1, replica_groups=mesh['member'=2,'gridy'=8,'gridx'=8] {'gridx'}, use_global_device_ids=true, to_apply=%region_37.38 | all-reduce | flops 512 | bytes 4096 | tf_op jit(solution)/shard_map/psum | solution.py:162
  1292.2 9.2 all_gather.10
  1301.4 20.8 %psum.159 = f32[2]{0:T(128)S(1)} all-reduce(f32[2]{0:T(128)S(1)} %broadcast_multiply_fusion.9), channel_id=1, replica_groups=mesh['member'=2,'gridy'=8,'gridx'=8] {'gridy'}, use_global_device_ids=true, to_apply=%region_40.41 | all-reduce | flops 2 | bytes 16 | tf_op jit(solution)/shard_map/psum | solution.py:164
  1323.0 5.8 all-reduce
  1331.9 8.0 all-gather.2.cloned.1.call-done
  1339.9 2.9 gather_fusion
  (333 shorter events, 115.2 us)
Async XLA Ops:
  7.2 1332.8 %all-gather.2.cloned.1.call-start = ((), (), s32[]{:S(2)}) async-start(), calls=%async_computation | async-start | bytes 6291456 | tf_op jit(solution)/shard_map/all_gather | solution.py:167
  11.0 29.6 %copy-start = (f32[5,2,4,64,256]{4,3,2,1,0:T(8,128)}, f32[5,2,4,64,256]{4,3,2,1,0:T(8,128)S(1)}, u32[]{:S(2)}) copy-start(f32[5,2,4,64,256]{4,3,2,1,0:T(8,128)S(1)} %constant_dynamic-update-slice_fusion) | copy-start | bytes 7864324
  11.0 4.3 collective-permute-start.1
  12.5 3.0 collective-permute-start
  14.2 23.5 %copy-start.44 = (f32[64]{0:T(128)}, f32[64]{0:T(128)S(1)}, u32[]{:S(2)}) copy-start(f32[64]{0:T(128)S(1)} %get-tuple-element.408) | copy-start | bytes 772
  19.9 14.3 %collective-permute-start.3 = (f32[5,2,4,66,1]{3,2,4,1,0:T(4,128)S(1)}, f32[5,2,4,66,1]{3,2,4,1,0:T(4,128)S(1)}, u32[]{:S(2)}, u32[]{:S(2)}) collective-permute-start(f32[5,2,4,66,1]{3,2,4,1,0:T(4,128)S(1)} %copy.16), channel_id=1, source_target_pairs={{0,1},{1,2},{2,3},{3,4},{4,5},{5,6},{6,7},{7,0},{8,9},{9,10},{10,1... | collective-permute-start | bytes 31688 | tf_op jit(solution)/shard_map/ppermute | solution.py:35
  23.1 12.9 collective-permute-start.2
  43.7 11.7 copy-start.25
  43.7 5.0 collective-permute-start.5
  47.9 1.2 collective-permute-start.4
  49.2 6.2 collective-permute-start.7
  49.3 6.9 collective-permute-start.6
  57.3 4.2 collective-permute-start.9
  60.7 1.2 collective-permute-start.8
  62.0 5.7 collective-permute-start.11
  62.1 5.7 collective-permute-start.10
  227.0 144.2 %copy-start.47 = (f32[2]{0:T(128)}, f32[2]{0:T(128)S(1)}, u32[]{:S(2)}) copy-start(f32[2]{0:T(128)S(1)} %div.41) | copy-start | bytes 28
  371.3 12.6 collective-permute-start.13
  383.0 1.2 collective-permute-start.12
  384.3 5.4 collective-permute-start.15
  384.4 5.6 collective-permute-start.14
  422.3 145.0 %copy-start.42 = (f32[2]{0:T(128)}, f32[2]{0:T(128)S(1)}, u32[]{:S(2)}) copy-start(f32[2]{0:T(128)S(1)} %div.43) | copy-start | bytes 28
  554.3 18.7 %copy-start.12 = (f32[2,64,256]{2,1,0:T(8,128)}, f32[2,64,256]{2,1,0:T(8,128)S(1)}, u32[]{:S(2)}) copy-start(f32[2,64,256]{2,1,0:T(8,128)S(1)} %multiply_add_fusion.4) | copy-start | bytes 393220
  554.3 12.6 collective-permute-start.17
  566.0 1.2 collective-permute-start.16
  567.3 5.4 collective-permute-start.19
  569.4 3.3 collective-permute-start.18
  611.8 13.5 copy-start.26
  611.8 8.0 collective-permute-start.20
  614.4 5.4 collective-permute-start.21
  619.9 5.4 collective-permute-start.23
  620.0 5.3 collective-permute-start.22
  626.0 38.2 %copy-start.16 = (f32[2,64,256]{2,1,0:T(8,128)}, f32[2,64,256]{2,1,0:T(8,128)S(1)}, u32[]{:S(2)}) copy-start(f32[2,64,256]{2,1,0:T(8,128)S(1)} %get-tuple-element.373) | copy-start | bytes 393220
  629.2 35.1 %copy-start.14 = (f32[2,64,256]{2,1,0:T(8,128)}, f32[2,64,256]{2,1,0:T(8,128)S(1)}, u32[]{:S(2)}) copy-start(f32[2,64,256]{2,1,0:T(8,128)S(1)} %subtract_multiply_fusion.4) | copy-start | bytes 393220
  630.6 5.0 collective-permute-start.25
  634.7 1.2 collective-permute-start.24
  641.0 15.0 %collective-permute-start.27 = (f32[5,2,4,66,1]{3,2,4,1,0:T(4,128)}, f32[5,2,4,66,1]{3,2,4,1,0:T(4,128)}, u32[]{:S(2)}, u32[]{:S(2)}) collective-permute-start(f32[5,2,4,66,1]{3,2,4,1,0:T(4,128)} %copy.20), channel_id=1, source_target_pairs={{0,1},{1,2},{2,3},{3,4},{4,5},{5,6},{6,7},{7,0},{8,9},{9,10},{10,1... | collective-permute-start | bytes 31688 | tf_op jit(solution)/shard_map/ppermute | solution.py:35
  643.5 14.9 %collective-permute-start.26 = (f32[5,2,4,66,1]{3,2,4,1,0:T(4,128)}, f32[5,2,4,66,1]{3,2,4,1,0:T(4,128)}, u32[]{:S(2)}, u32[]{:S(2)}) collective-permute-start(f32[5,2,4,66,1]{3,2,4,1,0:T(4,128)} %copy.18), channel_id=1, source_target_pairs={{1,0},{2,1},{3,2},{4,3},{5,4},{6,5},{7,6},{0,7},{9,8},{10,9},{11,1... | collective-permute-start | bytes 31688 | tf_op jit(solution)/shard_map/ppermute | solution.py:38
  664.3 12.3 copy-start.23
  667.4 10.2 copy-start.24
  667.4 4.6 collective-permute-start.29
  671.1 1.2 collective-permute-start.28
  673.1 7.3 collective-permute-start.31
  673.1 7.3 collective-permute-start.30
  681.8 4.5 collective-permute-start.33
  685.4 1.2 collective-permute-start.32
  687.3 7.5 collective-permute-start.35
  687.3 8.1 collective-permute-start.34
  1003.8 12.2 collective-permute-start.37
  1015.2 1.2 collective-permute-start.36
  1017.1 8.2 collective-permute-start.39
  1018.3 6.9 collective-permute-start.38
  1195.1 18.4 %copy-start.13 = (f32[2,64,256]{2,1,0:T(8,128)}, f32[2,64,256]{2,1,0:T(8,128)S(1)}, u32[]{:S(2)}) copy-start(f32[2,64,256]{2,1,0:T(8,128)S(1)} %multiply_add_fusion.1) | copy-start | bytes 393220
  1195.1 12.6 collective-permute-start.41
  1206.9 1.2 collective-permute-start.40
  1207.7 6.6 copy-start.37
  1208.8 8.2 collective-permute-start.43
  1210.8 6.2 collective-permute-start.42
  1251.9 10.9 copy-start.27
  1251.9 5.0 collective-permute-start.45
  1256.2 1.2 collective-permute-start.44
  1257.4 5.4 collective-permute-start.47
  1257.5 5.3 collective-permute-start.46
  1272.1 20.1 %copy-start.28 = (f32[2,64,256]{2,1,0:T(8,128)S(1)}, f32[2,64,256]{2,1,0:T(8,128)}, u32[]{:S(2)}) copy-start(f32[2,64,256]{2,1,0:T(8,128)} %copy-done.27) | copy-start | bytes 393220
  (38 other events, 119.3 us)
Sparse Core Ops, SparseCore 0:
  1273.7 66.1 all-gather.1
